TPU v7x, 512 devices: a whole 4x8x8 slice. The times are simulated.
512 devices in a mesh: band: 32 (over x, y_lo, core), grid: 16 (over z, y_hi).
Axes of the slice: x: 4, y: 8 (y_hi: 2, y_lo: 4; y = y_hi * 4 + y_lo), z: 8, core: 2. Of those that a mesh axis runs over, the one named last changes fastest.
Arguments:
- orbitals: bfloat16 [64, 160, 25600], P('band', 'grid'), may hold values from -6 to 6
- source_index: int32 [2], replicated, may hold values from 0 to 63
Outputs:
- fock_exchange: bfloat16 [64, 160, 25600], P('band', 'grid')
All inputs are finite; a program needn't handle non-finite values.
Results may differ from a plain program's by a relative error of at most 0.012.
The roundings to bfloat16 on the way count: a program that leaves them out, or rounds other values in their place, can miss the bound.
Values may be sent and summed in bfloat16 or wider, within the bound.
A program may use at most 64 MiB of HBM per device.

v0:
```python
import math

import jax
import jax.numpy as jnp
from jax import lax
from jax.sharding import PartitionSpec as P

spacing = 0.3


def broadcast(x, axis, root):
    mine = lax.axis_index(axis) == root
    return lax.psum(jnp.where(mine, x, jnp.zeros_like(x)), axis)


def cas_table(extent):
    wavenum = jnp.arange(extent, dtype=jnp.int32)
    products_mod = wavenum[:, None] * wavenum[None, :] % extent
    radians = products_mod.astype(jnp.float32) * (2.0 * math.pi / extent)
    return ((jnp.cos(radians) + jnp.sin(radians)) / math.sqrt(extent)).astype(jnp.bfloat16)


def wave_square(indices, extent):
    folded = jnp.minimum(indices, extent - indices).astype(jnp.float32)
    return folded * folded


def transform(grid_data, cas_matrix, pattern):
    return jnp.einsum(pattern, grid_data, cas_matrix, preferred_element_type=jnp.float32)


def potentials(pair_rho, cas_matrix, kernel_block):
    along_z = transform(pair_rho, cas_matrix, "pxyz,kz->pxyk").astype(jnp.bfloat16)
    along_y = transform(along_z, cas_matrix, "pxyz,ky->pxkz").astype(jnp.bfloat16)
    scaled = (
        kernel_block
        * transform(
            lax.all_to_all(along_y, "grid", split_axis=2, concat_axis=1, tiled=True),
            cas_matrix,
            "pxyz,kx->pkyz",
        )
    ).astype(jnp.bfloat16)
    back_x = transform(scaled, cas_matrix, "pxyz,kx->pkyz").astype(jnp.bfloat16)
    returned = lax.all_to_all(back_x, "grid", split_axis=1, concat_axis=2, tiled=True)
    again_y = transform(returned, cas_matrix, "pxyz,ky->pxkz").astype(jnp.bfloat16)
    return transform(again_y, cas_matrix, "pxyz,kz->pxyk")


def fetch_source(orbitals, which):
    local_count = orbitals.shape[0]
    local_slab = lax.dynamic_index_in_dim(orbitals, which % local_count, 0, keepdims=False)
    return broadcast(local_slab, "band", which // local_count)


def shards(orbitals, source_index):
    local_count = orbitals.shape[0]
    planes = orbitals.shape[1]
    extent = planes * lax.axis_size("grid")
    orbitals = orbitals.reshape(local_count, planes, extent, extent)
    source_count = source_index.shape[0]
    cas_matrix = cas_table(extent)
    columns = extent // lax.axis_size("grid")
    offset = lax.axis_index("grid") * columns
    square_x = wave_square(jnp.arange(extent, dtype=jnp.int32), extent)
    square_y = wave_square(offset + jnp.arange(columns, dtype=jnp.int32), extent)
    total_sq = square_x[:, None, None] + square_y[None, :, None] + square_x[None, None, :]
    strength = (extent * spacing) ** 2 / math.pi
    kernel_block = jnp.where(total_sq > 0, strength / (total_sq + 1.0), 0.0)
    fetched = None
    fetched = [fetch_source(orbitals, source_index[number]) for number in range(source_count)]
    stacked = jnp.stack(fetched)[:, None].astype(jnp.float32)
    pair_rho = (stacked * orbitals[None].astype(jnp.float32)).astype(jnp.bfloat16)
    pair_rho = pair_rho.reshape(source_count * local_count, planes, extent, extent)
    potential = potentials(pair_rho, cas_matrix, kernel_block)
    potential = potential.reshape(source_count, local_count, planes, extent, extent)
    summed_total = jnp.sum(stacked * potential, axis=0)
    result = (-summed_total).astype(jnp.bfloat16)
    return result.reshape(local_count, planes, extent * extent)


def solution(mesh):
    return jax.shard_map(
        shards,
        mesh=mesh,
        in_specs=(P("band", "grid", None), P()),
        out_specs=P("band", "grid", None),
        check_vma=False,
    )
```

profile of v0, /device:TPU:54, one launch (start us, length us, event | category | flops | bytes accessed | tf_op | source)
XLA Modules:
  0.0 598.6 jit_solution(17245803974825692510)
XLA Ops:
  6.5 0.0 all-reduce.3.cloned.1.call-start
  6.5 1.3 fusion.89
  13.0 3.7 reshape.107
  16.7 1.3 dynamic-slice_select_fusion.1
  18.0 0.0 all-reduce.3.cloned.1.call-update
  18.0 281.7 %all-reduce.3.cloned.1.call-done = (bf16[1,10,160,160]{3,2,0,1:T(8,128)(2,1)}, bf16[1,10,160,160]{3,2,0,1:T(8,128)(2,1)}) async-done(((bf16[1,10,160,160]{3,2,0,1:T(8,128)(2,1)}, bf16[1,10,160,160]{3,2,0,1:T(8,128)(2,1)}), (bf16[1,10,160,160]{3,2,0,1:T(8,128)(2,1)}, bf16[1,10,160,160]{3,2,0,1:T(8,128)(2,1)})) %all-reduce.3.cloned.1.call-update) | async-done | bytes 1024016 | tf_op jit(solution)/shard_map/psum | solution.py:13
  299.7 5.3 multiply_convert_fusion.1
  305.0 4.6 convert_bitcast_fusion.1
  309.6 4.2 copy.35
  313.8 12.8 %all-to-all-start = ((bf16[4,10,160,160]{3,0,1,2:T(4,128)(2,1)}), bf16[4,10,160,160]{3,0,1,2:T(4,128)(2,1)S(1)}, u32[]{:S(2)}, u32[]{:S(2)}) async-start(bf16[4,10,160,160]{3,0,1,2:T(4,128)(2,1)} %copy.35), calls=%async_computation | async-start | bytes 6553600 | tf_op jit(solution)/shard_map/all_to_all | solution.py:38
  326.6 0.1 broadcast_add_fusion
  326.7 1.6 fusion.30
  328.2 145.4 %all-to-all-done = bf16[4,10,160,160]{3,0,1,2:T(4,128)(2,1)S(1)} async-done(((bf16[4,10,160,160]{3,0,1,2:T(4,128)(2,1)}), bf16[4,10,160,160]{3,0,1,2:T(4,128)(2,1)S(1)}, u32[]{:S(2)}, u32[]{:S(2)}) %all-to-all-start) | async-done | bytes 2048032 | tf_op jit(solution)/shard_map/all_to_all | solution.py:38
  473.7 2.8 copy.37
  476.5 5.9 convert_bitcast_fusion
  482.3 2.5 copy.39
  484.9 90.1 %all_to_all.36 = bf16[4,160,10,160]{3,0,2,1:T(4,128)(2,1)S(1)} all-to-all(bf16[4,160,10,160]{3,0,2,1:T(4,128)(2,1)S(1)} %copy.39), channel_id=1, replica_groups=mesh['band'=32,'grid'=16] {'grid'}, dimensions={1} | all-to-all | bytes 4096000 | tf_op jit(solution)/shard_map/all_to_all | solution.py:44
  574.9 1.3 copy.40
  576.3 5.3 fusion.3
  581.5 5.0 multiply_reduce_fusion
  586.6 0.4 negate_convert_fusion
  587.0 2.7 reshape.112
  589.7 2.0 copy.45
  (2 shorter events, 0.0 us)
Async XLA Ops:
  6.5 293.2 %all-reduce.3.cloned.1.call-start = ((), (), s32[]{:S(2)}) async-start(), calls=%async_computation.2 | async-start | bytes 3276800 | tf_op jit(solution)/shard_map/psum | solution.py:13
  313.8 159.9 %all-to-all-start = ((bf16[4,10,160,160]{3,0,1,2:T(4,128)(2,1)}), bf16[4,10,160,160]{3,0,1,2:T(4,128)(2,1)S(1)}, u32[]{:S(2)}, u32[]{:S(2)}) async-start(bf16[4,10,160,160]{3,0,1,2:T(4,128)(2,1)} %copy.35), calls=%async_computation | async-start | bytes 6553600 | tf_op jit(solution)/shard_map/all_to_all | solution.py:38
Sparse Core Ops, SparseCore 0:
  18.1 281.5 all-reduce.2
where the time goes:
time: 599 us
  waiting for transfers between devices  427 us (71%)
  blocking collectives  90.1 us (15%)
  local copies, waits for them, and re-layouts  20.6 us (3%)
  between operations  18.5 us (3%)
  matrix products  15.7 us (3%)
  other arithmetic  13.7 us (2%)
  starting transfers between devices  12.8 us (2%)
    psum x1, waiting for transfers between devices, broadcast(): return lax.psum(jnp.where(mine, x, jnp.zeros_like(x)), axis)  282 us
    all_to_all x1, waiting for transfers between devices, potentials(): lax.all_to_all(along_y, 'grid', split_axis=2, concat_axis=1, tiled=True)  145 us
    all_to_all x1, blocking collectives, potentials(): lax.all_to_all(back_x, 'grid', split_axis=1, concat_axis=2, tiled=True)  90.1 us
    dot_general x3, matrix products, transform(): jnp.einsum(pattern, grid_data, cas_matrix, preferred_element_type=jnp.flo...  15.7 us
    all_to_all x1, starting transfers between devices, potentials(): lax.all_to_all(along_y, 'grid', split_axis=2, concat_axis=1, tiled=True)  12.8 us
  transfers between devices with their start and end apart: 2, of which 2 were waited for; matrix products, arithmetic and copies ran while one was open for 0% of the time, Pallas kernels for 0%

commit v1 on v0

v1 whole, which is shorter than its diff:
```python
import functools
import math

import jax
import jax.numpy as jnp
import ml_dtypes
import numpy as np
from jax import lax
from jax.experimental import pallas as pl
from jax.experimental.pallas import tpu as pltpu
from jax.sharding import PartitionSpec as P

MESH = pl.DeviceIdType.MESH
F32 = jnp.float32
BF16 = jnp.bfloat16

SPACING = 0.3
N = 160
NX = 10
NSRC = 2
NORB = 2
NGRID = 16
LANES = 128
REST = N - LANES
HALF = N // 2
GROUPS = N // 16
PAIRROWS = NX * 16
GRANULES = NORB * GROUPS + GROUPS // 2
SLAB = NX * N * N // LANES
PADDED = 2048
PIECE = PADDED // 8
STEP = 9


def tables():
    k = np.arange(N)
    radians = ((k[:, None] * k[None, :]) % N).astype(np.float32) * np.float32(2.0 * math.pi / N)
    cas = ((np.cos(radians) + np.sin(radians)) / np.float32(math.sqrt(N))).astype(ml_dtypes.bfloat16)
    cas = cas.astype(np.float32)
    order = np.array([4 * (r % 40) + r // 40 for r in range(N)])
    y_in = cas[:, order]
    y_out = cas[order, :]
    z_in = np.zeros((NORB, 4, 2, LANES, 2 * LANES), np.float32)
    z_out = np.zeros((NORB, 4, 2 * LANES, 2 * LANES), np.float32)
    for l in range(NORB):
        place = np.zeros((N, 2 * LANES), np.float32)
        place[:, :LANES] = cas[:, :LANES]
        for q in range(2):
            at = LANES + 64 * l + 32 * q
            place[:, at : at + REST] = cas[:, LANES:]
        back = np.zeros((2 * LANES, N), np.float32)
        back[:LANES] = cas[:LANES]
        back[LANES + 64 * l : LANES + 64 * l + REST] = cas[LANES:]
        for i in range(4):
            for part in range(2):
                for lane in range(LANES):
                    z = lane + LANES * (i + part) - N * i
                    if 0 <= z < N:
                        z_in[l, i, part, lane] = place[z]
                        z_out[l, i, :, LANES * part + lane] = back[:, z]
    return [t.astype(ml_dtypes.bfloat16) for t in (cas, y_in, y_out, z_in, z_out)]


def dot(a, b):
    return jnp.dot(a, b, preferred_element_type=F32)


def squares(index):
    folded = jnp.minimum(index, N - index).astype(F32)
    return folded * folded


def body(
    orb, con, cas, y_in, y_out, z_in, z_out, out,
    buf1, buf2, src, srcf, dens, srcd, mid, send, recv, work, ready, back, table, outf,
    s1, s2, s3, sf, sb, r1, r2, r3, rf, rb,
):
    band = lax.axis_index("band")
    me = lax.axis_index("grid")
    x_at = band // 8
    y_at = lax.rem(band // 2, 4)
    core = lax.rem(band, 2)
    q_me = x_at * 2 + core

    def at_q(q):
        return ((q // 2) * 8 + y_at * 2 + lax.rem(q, 2), me)

    def at_y(y):
        return (x_at * 8 + y * 2 + core, me)

    def at_grid(t):
        return (band, t)

    barrier = pltpu.get_barrier_semaphore()

    def hello(device):
        pl.semaphore_signal(barrier, inc=1, device_id=device, device_id_type=MESH)

    for k in range(1, 8):
        hello(at_q(lax.rem(q_me + k, 8)))
    for k in range(1, 4):
        hello(at_y(lax.rem(y_at + k, 4)))
    for k in range(1, NGRID):
        hello(at_grid(lax.rem(me + k, NGRID)))
    pl.semaphore_wait(barrier, 7 + 3 + NGRID - 1)

    def rows(q):
        return pl.ds(pl.multiple_of(q * PIECE, PIECE), PIECE)

    def first(j, k):
        q = lax.rem(q_me + k, 8)
        return pltpu.make_async_remote_copy(
            con.at[j, rows(q)], buf1.at[j, q_me], s1.at[j, k], r1.at[j],
            device_id=at_q(q), device_id_type=MESH)

    def second(j, k):
        y = lax.rem(y_at + k, 4)
        return pltpu.make_async_remote_copy(
            buf2.at[j, y_at], buf2.at[j, y_at], s2.at[j, k], r2.at[j],
            device_id=at_y(y), device_id_type=MESH)

    def third(j, k):
        q = lax.rem(q_me + k, 8)
        return pltpu.make_async_remote_copy(
            src.at[j, rows(q_me)], src.at[j, rows(q_me)], s3.at[j, k], r3.at[j],
            device_id=at_q(q), device_id_type=MESH)

    for j in range(NSRC):
        for k in range(1, 8):
            first(j, k).start()
    for j in range(NSRC):
        buf1[j, q_me] = con[j, rows(q_me), :]

    def granule(j, slot):
        return lax.rem(me + (NGRID - STEP) * j, NGRID) + NGRID * slot

    lane = lax.broadcasted_iota(jnp.int32, (1, LANES), 1)
    kx = squares(lax.broadcasted_iota(jnp.int32, (N, LANES), 0))
    strength = (N * SPACING) ** 2 / math.pi
    for j in range(NSRC):
        for slot in range(2):
            g = granule(j, slot)

            def fill(r, _, g=g, at=2 * j + slot):
                plain = jnp.zeros((1, LANES), jnp.int32) + (16 * lax.rem(g, GROUPS) + r)
                folded = HALF * lax.rem(lane // 32, 2) + (16 * (g - NORB * GROUPS) + r)
                rest = g >= NORB * GROUPS
                ky = jnp.where(rest, folded, plain)
                kz = jnp.where(rest, LANES + lax.rem(lane, 32), lane)
                total = kx + (squares(ky) + squares(kz))
                table[at, r] = jnp.where(total > 0, strength / (total + 1.0), 0.0)
                return 0

            lax.fori_loop(0, 16, fill, 0)

    for j in range(NSRC):
        got = buf1.at[j, pl.ds(0, 7)]
        pltpu.make_async_copy(got, got, r1.at[j]).wait()
        buf2[j, y_at] = jnp.sum(buf1[j].astype(F32), axis=0).astype(BF16)
        for k in range(1, 4):
            second(j, k).start()
    for j in range(NSRC):
        got = buf2.at[j, pl.ds(0, 3)]
        pltpu.make_async_copy(got, got, r2.at[j]).wait()
        src[j, rows(q_me), :] = jnp.sum(buf2[j].astype(F32), axis=0).astype(BF16)
        for k in range(1, 8):
            third(j, k).start()

    zone = lax.rem(lane // 32, 2) == 0

    def order(j, k):
        g = lax.rem(7 * k + 3 * me + 12 * core, GRANULES)
        t = lax.rem(g + STEP * j, NGRID)
        return g, t

    def forward(j, k):
        g, t = order(j, k)
        return t, pltpu.make_async_remote_copy(
            send.at[j, g], recv.at[j, g // NGRID, me], sf.at[j, k], rf.at[j, g // NGRID],
            device_id=at_grid(t), device_id_type=MESH)

    def forward_own(j, k):
        g, t = order(j, k)
        return pltpu.make_async_copy(send.at[j, g], recv.at[j, g // NGRID, me], rf.at[j, g // NGRID])

    for j in range(NSRC):
        got = src.at[j, pl.ds(0, 7 * PIECE)]
        pltpu.make_async_copy(got, got, r3.at[j]).wait()
        srcf[...] = src[j].astype(F32)

        def spread(x, _, j=j):
            at = pl.ds(pl.multiple_of(x * 40, 8), 40)
            for m in range(5):
                s = srcf[pl.ds(x * 200 + m, 40, stride=5), :]
                srcd[j, m, at, :] = s
                for l in range(NORB):
                    dens[l, m, at, :] = s * orb[l, pl.ds(x * 200 + m, 40, stride=5), :]
            return 0

        lax.fori_loop(0, NX, spread, 0)
        for i in range(4):
            parts = []
            for l in range(NORB):
                t = dot(dens[l, i].astype(BF16), z_in[l, i, 0]) + dot(dens[l, i + 1].astype(BF16), z_in[l, i, 1])
                mid[l, i] = t[:, :LANES]
                parts.append(t[:, LANES:])
            mid[NORB, i] = parts[0] + parts[1]

        def along_y(x, _, j=j):
            at = pl.ds(pl.multiple_of(x * 40, 8), 40)
            to = pl.ds(pl.multiple_of(x * 16, 16), 16)
            cols = [
                jnp.concatenate([mid[l, i, at, :] for i in range(4)], axis=0).astype(BF16)
                for l in range(NORB + 1)
            ]
            o = dot(y_in[...], jnp.concatenate(cols, axis=1))
            for l in range(NORB):
                for g in range(GROUPS):
                    send[j, l * GROUPS + g, to, :] = o[16 * g : 16 * g + 16, LANES * l : LANES * (l + 1)].astype(BF16)
            last = o[:, NORB * LANES :]
            both = jnp.where(zone, last[:HALF], last[HALF:])
            for g in range(GROUPS // 2):
                send[j, NORB * GROUPS + g, to, :] = both[16 * g : 16 * g + 16].astype(BF16)
            return 0

        lax.fori_loop(0, NX, along_y, 0)

        def post(k, _, j=j):
            t, copy = forward(j, k)

            @pl.when(t == me)
            def _():
                forward_own(j, k).start()

            @pl.when(t != me)
            def _():
                copy.start()

            return 0

        lax.fori_loop(0, GRANULES, post, 0)

    def reply(j, slot, k):
        t = lax.rem(me + k, NGRID)
        return pltpu.make_async_remote_copy(
            ready.at[j, slot, t], back.at[j, granule(j, slot)], sb.at[j, slot, k], rb.at[j],
            device_id=at_grid(t), device_id_type=MESH)

    def reply_own(j, slot):
        return pltpu.make_async_copy(ready.at[j, slot, me], back.at[j, granule(j, slot)], rb.at[j])

    def along_x(j, slot):
        got = recv.at[j, slot]
        pltpu.make_async_copy(got, got, rf.at[j, slot]).wait()
        work[...] = recv[j, slot].reshape(NGRID * PAIRROWS, LANES).astype(F32)

        def two(h, _):
            one = pl.ds(2 * h, N, stride=16)
            other = pl.ds(2 * h + 1, N, stride=16)
            f = jnp.concatenate([work[one, :].astype(BF16), work[other, :].astype(BF16)], axis=1)
            u = dot(cas[...], f)
            scale = jnp.concatenate([table[2 * j + slot, 2 * h], table[2 * j + slot, 2 * h + 1]], axis=1)
            v = dot(cas[...], (scale * u).astype(BF16))
            work[one, :] = v[:, :LANES]
            work[other, :] = v[:, LANES:]
            return 0

        lax.fori_loop(0, 8, two, 0)
        ready[j, slot] = work[...].astype(BF16).reshape(NGRID, PAIRROWS, LANES)
        reply_own(j, slot).start()
        for k in range(1, NGRID):
            reply(j, slot, k).start()

    for j in range(NSRC):
        along_x(j, 0)

        @pl.when(granule(j, 1) < GRANULES)
        def _(j=j):
            along_x(j, 1)

    for j in range(NSRC):
        got = back.at[j]
        pltpu.make_async_copy(got, got, rb.at[j]).wait()

        def again_y(x, _, j=j):
            at = pl.ds(pl.multiple_of(x * 40, 8), 40)
            to = pl.ds(pl.multiple_of(x * 16, 16), 16)
            cols = [back[j, pl.ds(l * GROUPS, GROUPS), to, :].reshape(N, LANES) for l in range(NORB)]
            b = back[j, pl.ds(NORB * GROUPS, GROUPS // 2), to, :].reshape(HALF, LANES)
            turned = pltpu.roll(b.astype(F32), LANES - 32, 1).astype(BF16)
            cols.append(jnp.concatenate([b, turned], axis=0))
            o = dot(y_out[...], jnp.concatenate(cols, axis=1))
            for l in range(NORB + 1):
                for i in range(4):
                    mid[l, i, at, :] = o[40 * i : 40 * i + 40, LANES * l : LANES * (l + 1)]
            return 0

        lax.fori_loop(0, NX, again_y, 0)
        for l in range(NORB):
            left = None
            for i in range(4):
                f = jnp.concatenate([mid[l, i].astype(BF16), mid[NORB, i].astype(BF16)], axis=1)
                t = dot(f, z_out[l, i])
                here = t[:, :LANES] if left is None else left + t[:, :LANES]
                left = t[:, LANES:]
                dens[l, i] = srcd[j, i] * here if j == 0 else dens[l, i] + srcd[j, i] * here
            dens[l, 4] = srcd[j, 4] * left if j == 0 else dens[l, 4] + srcd[j, 4] * left

    def gather(x, _):
        at = pl.ds(pl.multiple_of(x * 40, 8), 40)
        for l in range(NORB):
            for m in range(5):
                outf[l, pl.ds(x * 200 + m, 40, stride=5), :] = -dens[l, m, at, :]
        return 0

    lax.fori_loop(0, NX, gather, 0)
    out[...] = outf[...].astype(BF16)

    for j in range(NSRC):
        for k in range(1, 8):
            first(j, k).wait_send()
            third(j, k).wait_send()
        for k in range(1, 4):
            second(j, k).wait_send()

        def posted(k, _, j=j):
            t, copy = forward(j, k)

            @pl.when(t != me)
            def _():
                copy.wait_send()

            return 0

        lax.fori_loop(0, GRANULES, posted, 0)
        for slot in range(2):

            @pl.when(granule(j, slot) < GRANULES)
            def _(j=j, slot=slot):
                for k in range(1, NGRID):
                    reply(j, slot, k).wait_send()


def exchange(orb, con):
    consts = [jnp.asarray(t) for t in tables()]
    vmem = pl.BlockSpec(memory_space=pltpu.VMEM)
    dma = pltpu.SemaphoreType.DMA
    return pl.pallas_call(
        body,
        out_shape=jax.ShapeDtypeStruct((NORB, SLAB, LANES), BF16),
        in_specs=[vmem] * (2 + len(consts)),
        out_specs=vmem,
        scratch_shapes=[
            pltpu.VMEM((NSRC, 8, PIECE, LANES), BF16),
            pltpu.VMEM((NSRC, 4, PIECE, LANES), BF16),
            pltpu.VMEM((NSRC, PADDED, LANES), BF16),
            pltpu.VMEM((PADDED, LANES), F32),
            pltpu.VMEM((NORB, 5, 40 * NX, LANES), F32),
            pltpu.VMEM((NSRC, 5, 40 * NX, LANES), F32),
            pltpu.VMEM((NORB + 1, 4, 40 * NX, LANES), F32),
            pltpu.VMEM((NSRC, GRANULES, PAIRROWS, LANES), BF16),
            pltpu.VMEM((NSRC, 2, NGRID, PAIRROWS, LANES), BF16),
            pltpu.VMEM((NGRID * PAIRROWS, LANES), F32),
            pltpu.VMEM((NSRC, 2, NGRID, PAIRROWS, LANES), BF16),
            pltpu.VMEM((NSRC, GRANULES, PAIRROWS, LANES), BF16),
            pltpu.VMEM((2 * NSRC, 16, N, LANES), F32),
            pltpu.VMEM((NORB, SLAB, LANES), F32),
            dma((NSRC, 8)),
            dma((NSRC, 4)),
            dma((NSRC, 8)),
            dma((NSRC, GRANULES)),
            dma((NSRC, 2, NGRID)),
            dma((NSRC,)),
            dma((NSRC,)),
            dma((NSRC,)),
            dma((NSRC, 2)),
            dma((NSRC,)),
        ],
        compiler_params=pltpu.CompilerParams(
            collective_id=0, has_side_effects=True, vmem_limit_bytes=56 << 20
        ),
        name="exchange",
    )(orb, con, *consts)


def shards(orbitals, source_index):
    local = orbitals.shape[0]
    flat = orbitals.reshape(local, SLAB, LANES)
    band = lax.axis_index("band")
    parts = []
    for j in range(NSRC):
        slab = lax.dynamic_index_in_dim(flat, source_index[j] % local, 0, keepdims=False)
        parts.append(jnp.where(band == source_index[j] // local, slab, jnp.zeros_like(slab)))
    con = jnp.pad(jnp.stack(parts), ((0, 0), (0, PADDED - SLAB), (0, 0)))
    result = exchange(flat.astype(F32), con)
    return result.reshape(orbitals.shape)


def solution(mesh):
    return jax.shard_map(
        shards,
        mesh=mesh,
        in_specs=(P("band", "grid", None), P()),
        out_specs=P("band", "grid", None),
        check_vma=False,
    )
```

time: 599 us -> 186 us (0.31)
  the two profiles are of different devices: /device:TPU:54 before, /device:TPU:28 now
where the time goes in v1:
time: 186 us
  Pallas kernels  171 us (92%)
  local copies, waits for them, and re-layouts  7.16 us (4%)
  between operations  5.23 us (3%)
  other arithmetic  2.68 us (1%)
    pallas_call x1, Pallas kernels, exchange(): pl.pallas_call(body, out_shape=jax.ShapeDtypeStruct((NORB, SLAB, LANES),...  171 us

profile of v1, /device:TPU:28, one launch (start us, length us, event | category | flops | bytes accessed | tf_op | source)
XLA Modules:
  0.0 186.1 jit_solution(2159793557189284219)
XLA Ops:
  0.0 1.3 fusion.3
  6.5 1.4 copy.10
  8.0 0.7 reshape.6
  8.7 0.1 dynamic-slice_select_fusion.1
  8.8 1.1 fusion.2.con
  9.9 1.5 convert_element_type.5.orb
  11.4 171.0 %exchange.1 = bf16[2,2000,128]{2,1,0:T(8,128)(2,1)} custom-call(f32[2,2000,128]{2,1,0:T(8,128)} %convert_element_type.5.orb, bf16[2,2048,128]{2,1,0:T(8,128)(2,1)} %fusion.2.con, bf16[160,160]{1,0:T(8,128)(2,1)} %constant.61.clone.cas, bf16[160,160]{1,0:T(8,128)(2,1)} %constant.62.clone.y_in, bf16[160,160]{1,0:T(8,128)(2,1)} %constant.63.clone.y_out, ...), custom_call_target="tpu_custom_call" | custom-call | tf_op jit(solution)/shard_map/exchange/pallas_call | solution.py:348
  182.4 1.6 reshape.7
  184.1 2.0 %copy.11 = bf16[2,10,25600]{2,0,1:T(2,128)(2,1)} copy(bf16[2,10,25600]{2,1,0:T(8,128)(2,1)S(1)} %reshape.7) | data formatting | bytes 2048000 | tf_op jit(solution)/shard_map/reshape | solution.py:396

commit v2 on v1

--- a/solution.py
+++ b/solution.py
@@ -1,4 +1,3 @@
-import functools
 import math
 
 import jax
@@ -71,8 +70,8 @@
 
 
 def body(
-    orb, con, cas, y_in, y_out, z_in, z_out, out,
-    buf1, buf2, src, srcf, dens, srcd, mid, send, recv, work, ready, back, table, outf,
+    index, orb, cas, y_in, y_out, z_in, z_out, out,
+    flat, con, buf1, buf2, src, srcf, dens, srcd, mid, send, recv, work, ready, back, table,
     s1, s2, s3, sf, sb, r1, r2, r3, rf, rb,
 ):
     band = lax.axis_index("band")
@@ -102,34 +101,20 @@
         hello(at_y(lax.rem(y_at + k, 4)))
     for k in range(1, NGRID):
         hello(at_grid(lax.rem(me + k, NGRID)))
-    pl.semaphore_wait(barrier, 7 + 3 + NGRID - 1)
-
-    def rows(q):
-        return pl.ds(pl.multiple_of(q * PIECE, PIECE), PIECE)
-
-    def first(j, k):
-        q = lax.rem(q_me + k, 8)
-        return pltpu.make_async_remote_copy(
-            con.at[j, rows(q)], buf1.at[j, q_me], s1.at[j, k], r1.at[j],
-            device_id=at_q(q), device_id_type=MESH)
-
-    def second(j, k):
-        y = lax.rem(y_at + k, 4)
-        return pltpu.make_async_remote_copy(
-            buf2.at[j, y_at], buf2.at[j, y_at], s2.at[j, k], r2.at[j],
-            device_id=at_y(y), device_id_type=MESH)
-
-    def third(j, k):
-        q = lax.rem(q_me + k, 8)
-        return pltpu.make_async_remote_copy(
-            src.at[j, rows(q_me)], src.at[j, rows(q_me)], s3.at[j, k], r3.at[j],
-            device_id=at_q(q), device_id_type=MESH)
-
-    for j in range(NSRC):
-        for k in range(1, 8):
-            first(j, k).start()
-    for j in range(NSRC):
-        buf1[j, q_me] = con[j, rows(q_me), :]
+
+    flat[...] = orb[...].astype(F32).reshape(NORB * SLAB, LANES)
+    for j in range(NSRC):
+        mine = [jnp.where(index[j] == NORB * band + l, 1.0, 0.0) for l in range(NORB)]
+
+        def share(h, _, j=j, mine=mine):
+            part = sum(
+                mine[l] * flat[pl.ds(h * NORB * 400 + l, 400, stride=NORB), :] for l in range(NORB)
+            )
+            con[j, pl.ds(pl.multiple_of(h * 400, 16), 400), :] = part.astype(BF16)
+            return 0
+
+        lax.fori_loop(0, SLAB // 400, share, 0)
+        con[j, SLAB:, :] = jnp.zeros((PADDED - SLAB, LANES), BF16)
 
     def granule(j, slot):
         return lax.rem(me + (NGRID - STEP) * j, NGRID) + NGRID * slot
@@ -153,23 +138,62 @@
 
             lax.fori_loop(0, 16, fill, 0)
 
-    for j in range(NSRC):
+    pl.semaphore_wait(barrier, 7 + 3 + NGRID - 1)
+
+    def rows(q):
+        return pl.ds(pl.multiple_of(q * PIECE, PIECE), PIECE)
+
+    def first(j, k):
+        q = lax.rem(q_me + k, 8)
+        return pltpu.make_async_remote_copy(
+            con.at[j, rows(q)], buf1.at[j, q_me], s1.at[j, k], r1.at[j],
+            device_id=at_q(q), device_id_type=MESH)
+
+    def second(j, k):
+        y = lax.rem(y_at + k, 4)
+        return pltpu.make_async_remote_copy(
+            buf2.at[j, y_at], buf2.at[j, y_at], s2.at[j, k], r2.at[j],
+            device_id=at_y(y), device_id_type=MESH)
+
+    def third(j, k):
+        q = lax.rem(q_me + k, 8)
+        return pltpu.make_async_remote_copy(
+            src.at[j, rows(q_me)], src.at[j, rows(q_me)], s3.at[j, k], r3.at[j],
+            device_id=at_q(q), device_id_type=MESH)
+
+    def begin(j):
+        for k in range(1, 8):
+            first(j, k).start()
+        buf1[j, q_me] = con[j, rows(q_me), :]
+
+    def middle(j):
         got = buf1.at[j, pl.ds(0, 7)]
         pltpu.make_async_copy(got, got, r1.at[j]).wait()
         buf2[j, y_at] = jnp.sum(buf1[j].astype(F32), axis=0).astype(BF16)
         for k in range(1, 4):
             second(j, k).start()
-    for j in range(NSRC):
+
+    def end(j):
         got = buf2.at[j, pl.ds(0, 3)]
         pltpu.make_async_copy(got, got, r2.at[j]).wait()
         src[j, rows(q_me), :] = jnp.sum(buf2[j].astype(F32), axis=0).astype(BF16)
         for k in range(1, 8):
             third(j, k).start()
 
+    begin(0)
+    middle(0)
+    begin(1)
+    end(0)
+    middle(1)
+    end(1)
+
     zone = lax.rem(lane // 32, 2) == 0
 
     def order(j, k):
-        g = lax.rem(7 * k + 3 * me + 12 * core, GRANULES)
+        turn = 2 * me + 5 * core + 3 * y_at
+        low = lax.rem(7 * k + turn, NGRID)
+        high = NGRID + lax.rem(2 * k + turn, GRANULES - NGRID)
+        g = jnp.where(k < NGRID, low, high)
         t = lax.rem(g + STEP * j, NGRID)
         return g, t
 
@@ -194,7 +218,7 @@
                 s = srcf[pl.ds(x * 200 + m, 40, stride=5), :]
                 srcd[j, m, at, :] = s
                 for l in range(NORB):
-                    dens[l, m, at, :] = s * orb[l, pl.ds(x * 200 + m, 40, stride=5), :]
+                    dens[l, m, at, :] = s * flat[pl.ds(NORB * (x * 200 + m) + l, 40, stride=5 * NORB), :]
             return 0
 
         lax.fori_loop(0, NX, spread, 0)
@@ -241,8 +265,8 @@
         lax.fori_loop(0, GRANULES, post, 0)
 
     def reply(j, slot, k):
-        t = lax.rem(me + k, NGRID)
-        return pltpu.make_async_remote_copy(
+        t = lax.rem(7 * k + 2 * me + 5 * core + 3 * y_at, NGRID)
+        return t, pltpu.make_async_remote_copy(
             ready.at[j, slot, t], back.at[j, granule(j, slot)], sb.at[j, slot, k], rb.at[j],
             device_id=at_grid(t), device_id_type=MESH)
 
@@ -267,9 +291,21 @@
 
         lax.fori_loop(0, 8, two, 0)
         ready[j, slot] = work[...].astype(BF16).reshape(NGRID, PAIRROWS, LANES)
-        reply_own(j, slot).start()
-        for k in range(1, NGRID):
-            reply(j, slot, k).start()
+
+        def answer(k, _):
+            t, copy = reply(j, slot, k)
+
+            @pl.when(t == me)
+            def _():
+                reply_own(j, slot).start()
+
+            @pl.when(t != me)
+            def _():
+                copy.start()
+
+            return 0
+
+        lax.fori_loop(0, NGRID, answer, 0)
 
     for j in range(NSRC):
         along_x(j, 0)
@@ -310,11 +346,11 @@
         at = pl.ds(pl.multiple_of(x * 40, 8), 40)
         for l in range(NORB):
             for m in range(5):
-                outf[l, pl.ds(x * 200 + m, 40, stride=5), :] = -dens[l, m, at, :]
+                flat[pl.ds(NORB * (x * 200 + m) + l, 40, stride=5 * NORB), :] = -dens[l, m, at, :]
         return 0
 
     lax.fori_loop(0, NX, gather, 0)
-    out[...] = outf[...].astype(BF16)
+    out[...] = flat[...].reshape(SLAB, NORB, LANES).astype(BF16)
 
     for j in range(NSRC):
         for k in range(1, 8):
@@ -337,20 +373,30 @@
 
             @pl.when(granule(j, slot) < GRANULES)
             def _(j=j, slot=slot):
-                for k in range(1, NGRID):
-                    reply(j, slot, k).wait_send()
-
-
-def exchange(orb, con):
+                def answered(k, _):
+                    t, copy = reply(j, slot, k)
+
+                    @pl.when(t != me)
+                    def _():
+                        copy.wait_send()
+
+                    return 0
+
+                lax.fori_loop(0, NGRID, answered, 0)
+
+
+def exchange(index, orb):
     consts = [jnp.asarray(t) for t in tables()]
     vmem = pl.BlockSpec(memory_space=pltpu.VMEM)
     dma = pltpu.SemaphoreType.DMA
     return pl.pallas_call(
         body,
-        out_shape=jax.ShapeDtypeStruct((NORB, SLAB, LANES), BF16),
-        in_specs=[vmem] * (2 + len(consts)),
+        out_shape=jax.ShapeDtypeStruct((SLAB, NORB, LANES), BF16),
+        in_specs=[pl.BlockSpec(memory_space=pltpu.SMEM)] + [vmem] * (1 + len(consts)),
         out_specs=vmem,
         scratch_shapes=[
+            pltpu.VMEM((NORB * SLAB, LANES), F32),
+            pltpu.VMEM((NSRC, PADDED, LANES), BF16),
             pltpu.VMEM((NSRC, 8, PIECE, LANES), BF16),
             pltpu.VMEM((NSRC, 4, PIECE, LANES), BF16),
             pltpu.VMEM((NSRC, PADDED, LANES), BF16),
@@ -364,7 +410,6 @@
             pltpu.VMEM((NSRC, 2, NGRID, PAIRROWS, LANES), BF16),
             pltpu.VMEM((NSRC, GRANULES, PAIRROWS, LANES), BF16),
             pltpu.VMEM((2 * NSRC, 16, N, LANES), F32),
-            pltpu.VMEM((NORB, SLAB, LANES), F32),
             dma((NSRC, 8)),
             dma((NSRC, 4)),
             dma((NSRC, 8)),
@@ -380,20 +425,13 @@
             collective_id=0, has_side_effects=True, vmem_limit_bytes=56 << 20
         ),
         name="exchange",
-    )(orb, con, *consts)
+    )(index, orb, *consts)
 
 
 def shards(orbitals, source_index):
-    local = orbitals.shape[0]
-    flat = orbitals.reshape(local, SLAB, LANES)
-    band = lax.axis_index("band")
-    parts = []
-    for j in range(NSRC):
-        slab = lax.dynamic_index_in_dim(flat, source_index[j] % local, 0, keepdims=False)
-        parts.append(jnp.where(band == source_index[j] // local, slab, jnp.zeros_like(slab)))
-    con = jnp.pad(jnp.stack(parts), ((0, 0), (0, PADDED - SLAB), (0, 0)))
-    result = exchange(flat.astype(F32), con)
-    return result.reshape(orbitals.shape)
+    rows = orbitals.reshape(NORB, SLAB, LANES).transpose(1, 0, 2)
+    result = exchange(source_index, rows)
+    return result.transpose(1, 0, 2).reshape(orbitals.shape)
 
 
 def solution(mesh):

time: 186 us -> 164 us (0.88)
  the two profiles are of different devices: /device:TPU:28 before, /device:TPU:10 now
where the time goes in v2:
time: 164 us
  Pallas kernels  161 us (98%)
  local copies, waits for them, and re-layouts  2.88 us (2%)
    pallas_call x1, Pallas kernels, exchange(): pl.pallas_call(body, out_shape=jax.ShapeDtypeStruct((SLAB, NORB, LANES),...  161 us

profile of v2, /device:TPU:10, one launch (start us, length us, event | category | flops | bytes accessed | tf_op | source)
XLA Modules:
  0.0 163.7 jit_solution(16399958243643927769)
XLA Ops:
  0.0 160.8 %exchange.1 = bf16[2000,2,128]{2,1,0:T(2,128)(2,1)} custom-call(s32[2]{0:T(128)} %index.1, bf16[2000,2,128]{2,1,0:T(2,128)(2,1)} %bitcast.7, bf16[160,160]{1,0:T(8,128)(2,1)} %constant.10.clone.cas, bf16[160,160]{1,0:T(8,128)(2,1)} %constant.11.clone.y_in, bf16[160,160]{1,0:T(8,128)(2,1)} %constant.12.clone.y_out, ...), custom_call_target="tpu_custom_call" | custom-call | tf_op jit(solution)/shard_map/exchange/pallas_call | solution.py:392
  160.8 2.9 %copy.9 = bf16[2,10,25600]{2,0,1:T(2,128)(2,1)} copy(bf16[2,10,25600]{2,0,1:T(2,128)(2,1)} %bitcast.6) | data formatting | bytes 2048000

commit v3 on v2

--- a/solution.py
+++ b/solution.py
@@ -71,18 +71,19 @@
 
 def body(
     index, orb, cas, y_in, y_out, z_in, z_out, out,
-    flat, con, buf1, buf2, src, srcf, dens, srcd, mid, send, recv, work, ready, back, table,
-    s1, s2, s3, sf, sb, r1, r2, r3, rf, rb,
+    flat, orbd, con, bufd, pair, buf1, buf2, src, dens, total, mid, send, recv, work, ready, back, table,
+    sd, s1, s2, s3, se, sf, sb, rd, r1, r2, r3, re, rf, rb,
 ):
     band = lax.axis_index("band")
     me = lax.axis_index("grid")
     x_at = band // 8
     y_at = lax.rem(band // 2, 4)
     core = lax.rem(band, 2)
-    q_me = x_at * 2 + core
-
-    def at_q(q):
-        return ((q // 2) * 8 + y_at * 2 + lax.rem(q, 2), me)
+
+    def at_x(x):
+        return (x * 8 + y_at * 2 + core, me)
+
+    twin = (x_at * 8 + y_at * 2 + 1 - core, me)
 
     def at_y(y):
         return (x_at * 8 + y * 2 + core, me)
@@ -95,29 +96,100 @@
     def hello(device):
         pl.semaphore_signal(barrier, inc=1, device_id=device, device_id_type=MESH)
 
-    for k in range(1, 8):
-        hello(at_q(lax.rem(q_me + k, 8)))
+    hello(twin)
     for k in range(1, 4):
+        hello(at_x(lax.rem(x_at + k, 4)))
         hello(at_y(lax.rem(y_at + k, 4)))
     for k in range(1, NGRID):
         hello(at_grid(lax.rem(me + k, NGRID)))
 
     flat[...] = orb[...].astype(F32).reshape(NORB * SLAB, LANES)
+
+    def classes(x, _):
+        at = pl.ds(pl.multiple_of(x * 40, 8), 40)
+        for m in range(5):
+            for l in range(NORB):
+                orbd[l, m, at, :] = flat[pl.ds(NORB * (x * 200 + m) + l, 40, stride=5 * NORB), :]
+        return 0
+
+    lax.fori_loop(0, NX, classes, 0)
     for j in range(NSRC):
         mine = [jnp.where(index[j] == NORB * band + l, 1.0, 0.0) for l in range(NORB)]
 
-        def share(h, _, j=j, mine=mine):
-            part = sum(
-                mine[l] * flat[pl.ds(h * NORB * 400 + l, 400, stride=NORB), :] for l in range(NORB)
-            )
-            con[j, pl.ds(pl.multiple_of(h * 400, 16), 400), :] = part.astype(BF16)
-            return 0
-
-        lax.fori_loop(0, SLAB // 400, share, 0)
+        for m in range(5):
+            part = sum(mine[l] * orbd[l, m] for l in range(NORB))
+            con[j, 400 * m : 400 * m + 400, :] = part.astype(BF16)
         con[j, SLAB:, :] = jnp.zeros((PADDED - SLAB, LANES), BF16)
 
     def granule(j, slot):
         return lax.rem(me + (NGRID - STEP) * j, NGRID) + NGRID * slot
+
+    pl.semaphore_wait(barrier, 1 + 3 + 3 + NGRID - 1)
+
+    def half(c):
+        return pl.ds(pl.multiple_of(c * (PADDED // 2), PADDED // 2), PADDED // 2)
+
+    def piece(x):
+        return pl.ds(pl.multiple_of(x * PIECE, PIECE), PIECE)
+
+    own = pl.ds(pl.multiple_of(core * (PADDED // 2) + x_at * PIECE, PIECE), PIECE)
+
+    def swap(j):
+        return pltpu.make_async_remote_copy(
+            con.at[j, half(1 - core)], bufd.at[j], sd.at[j], rd.at[j], device_id=twin, device_id_type=MESH)
+
+    def first(j, k):
+        x = lax.rem(x_at + k, 4)
+        return pltpu.make_async_remote_copy(
+            pair.at[j, piece(x)], buf1.at[j, x_at], s1.at[j, k], r1.at[j],
+            device_id=at_x(x), device_id_type=MESH)
+
+    def second(j, k):
+        y = lax.rem(y_at + k, 4)
+        return pltpu.make_async_remote_copy(
+            buf2.at[j, y_at], buf2.at[j, y_at], s2.at[j, k], r2.at[j],
+            device_id=at_y(y), device_id_type=MESH)
+
+    def third(j, k):
+        x = lax.rem(x_at + k, 4)
+        return pltpu.make_async_remote_copy(
+            src.at[j, own], src.at[j, own], s3.at[j, k], r3.at[j],
+            device_id=at_x(x), device_id_type=MESH)
+
+    def give(j):
+        ours = src.at[j, half(core)]
+        return pltpu.make_async_remote_copy(
+            ours, ours, se.at[j], re.at[j], device_id=twin, device_id_type=MESH)
+
+    def along_x1(j):
+        swap(j).wait_recv()
+        pair[j] = (con[j, half(core), :].astype(F32) + bufd[j].astype(F32)).astype(BF16)
+        for k in range(1, 4):
+            first(j, k).start()
+        buf1[j, x_at] = pair[j, piece(x_at), :]
+
+    def along_y1(j):
+        got = buf1.at[j, pl.ds(0, 3)]
+        pltpu.make_async_copy(got, got, r1.at[j]).wait()
+        buf2[j, y_at] = jnp.sum(buf1[j].astype(F32), axis=0).astype(BF16)
+        for k in range(1, 4):
+            second(j, k).start()
+
+    def along_x2(j):
+        got = buf2.at[j, pl.ds(0, 3)]
+        pltpu.make_async_copy(got, got, r2.at[j]).wait()
+        src[j, own, :] = jnp.sum(buf2[j].astype(F32), axis=0).astype(BF16)
+        for k in range(1, 4):
+            third(j, k).start()
+
+    def to_twin(j):
+        got = src.at[j, pl.ds(0, 3 * PIECE)]
+        pltpu.make_async_copy(got, got, r3.at[j]).wait()
+        give(j).start()
+
+    swap(0).start()
+    swap(1).start()
+    along_x1(0)
 
     lane = lax.broadcasted_iota(jnp.int32, (1, LANES), 1)
     kx = squares(lax.broadcasted_iota(jnp.int32, (N, LANES), 0))
@@ -138,54 +210,12 @@
 
             lax.fori_loop(0, 16, fill, 0)
 
-    pl.semaphore_wait(barrier, 7 + 3 + NGRID - 1)
-
-    def rows(q):
-        return pl.ds(pl.multiple_of(q * PIECE, PIECE), PIECE)
-
-    def first(j, k):
-        q = lax.rem(q_me + k, 8)
-        return pltpu.make_async_remote_copy(
-            con.at[j, rows(q)], buf1.at[j, q_me], s1.at[j, k], r1.at[j],
-            device_id=at_q(q), device_id_type=MESH)
-
-    def second(j, k):
-        y = lax.rem(y_at + k, 4)
-        return pltpu.make_async_remote_copy(
-            buf2.at[j, y_at], buf2.at[j, y_at], s2.at[j, k], r2.at[j],
-            device_id=at_y(y), device_id_type=MESH)
-
-    def third(j, k):
-        q = lax.rem(q_me + k, 8)
-        return pltpu.make_async_remote_copy(
-            src.at[j, rows(q_me)], src.at[j, rows(q_me)], s3.at[j, k], r3.at[j],
-            device_id=at_q(q), device_id_type=MESH)
-
-    def begin(j):
-        for k in range(1, 8):
-            first(j, k).start()
-        buf1[j, q_me] = con[j, rows(q_me), :]
-
-    def middle(j):
-        got = buf1.at[j, pl.ds(0, 7)]
-        pltpu.make_async_copy(got, got, r1.at[j]).wait()
-        buf2[j, y_at] = jnp.sum(buf1[j].astype(F32), axis=0).astype(BF16)
-        for k in range(1, 4):
-            second(j, k).start()
-
-    def end(j):
-        got = buf2.at[j, pl.ds(0, 3)]
-        pltpu.make_async_copy(got, got, r2.at[j]).wait()
-        src[j, rows(q_me), :] = jnp.sum(buf2[j].astype(F32), axis=0).astype(BF16)
-        for k in range(1, 8):
-            third(j, k).start()
-
-    begin(0)
-    middle(0)
-    begin(1)
-    end(0)
-    middle(1)
-    end(1)
+    along_y1(0)
+    along_x1(1)
+    along_x2(0)
+    along_y1(1)
+    to_twin(0)
+    along_x2(1)
 
     zone = lax.rem(lane // 32, 2) == 0
 
@@ -208,46 +238,32 @@
         return pltpu.make_async_copy(send.at[j, g], recv.at[j, g // NGRID, me], rf.at[j, g // NGRID])
 
     for j in range(NSRC):
-        got = src.at[j, pl.ds(0, 7 * PIECE)]
-        pltpu.make_async_copy(got, got, r3.at[j]).wait()
-        srcf[...] = src[j].astype(F32)
-
-        def spread(x, _, j=j):
+        if j == 1:
+            to_twin(1)
+        give(j).wait_recv()
+        for m in range(5):
+            wide = src[j, 400 * m : 400 * m + 400, :].astype(F32)
+            for l in range(NORB):
+                dens[l, m] = (wide * orbd[l, m]).astype(BF16)
+
+        def along_z(l):
+            for i in range(4):
+                t = dot(dens[l, i], z_in[l, i, 0]) + dot(dens[l, i + 1], z_in[l, i, 1])
+                mid[l, i] = t[:, :LANES]
+                mid[NORB, i] = t[:, LANES:] if l == 0 else mid[NORB, i] + t[:, LANES:]
+
+        def along_y(x, which):
             at = pl.ds(pl.multiple_of(x * 40, 8), 40)
-            for m in range(5):
-                s = srcf[pl.ds(x * 200 + m, 40, stride=5), :]
-                srcd[j, m, at, :] = s
-                for l in range(NORB):
-                    dens[l, m, at, :] = s * flat[pl.ds(NORB * (x * 200 + m) + l, 40, stride=5 * NORB), :]
-            return 0
-
-        lax.fori_loop(0, NX, spread, 0)
-        for i in range(4):
-            parts = []
-            for l in range(NORB):
-                t = dot(dens[l, i].astype(BF16), z_in[l, i, 0]) + dot(dens[l, i + 1].astype(BF16), z_in[l, i, 1])
-                mid[l, i] = t[:, :LANES]
-                parts.append(t[:, LANES:])
-            mid[NORB, i] = parts[0] + parts[1]
-
-        def along_y(x, _, j=j):
-            at = pl.ds(pl.multiple_of(x * 40, 8), 40)
-            to = pl.ds(pl.multiple_of(x * 16, 16), 16)
             cols = [
                 jnp.concatenate([mid[l, i, at, :] for i in range(4)], axis=0).astype(BF16)
-                for l in range(NORB + 1)
+                for l in which
             ]
-            o = dot(y_in[...], jnp.concatenate(cols, axis=1))
-            for l in range(NORB):
-                for g in range(GROUPS):
-                    send[j, l * GROUPS + g, to, :] = o[16 * g : 16 * g + 16, LANES * l : LANES * (l + 1)].astype(BF16)
-            last = o[:, NORB * LANES :]
-            both = jnp.where(zone, last[:HALF], last[HALF:])
-            for g in range(GROUPS // 2):
-                send[j, NORB * GROUPS + g, to, :] = both[16 * g : 16 * g + 16].astype(BF16)
-            return 0
-
-        lax.fori_loop(0, NX, along_y, 0)
+            return dot(y_in[...], jnp.concatenate(cols, axis=1) if len(cols) > 1 else cols[0])
+
+        def store(l, x, o, j=j):
+            to = pl.ds(pl.multiple_of(x * 16, 16), 16)
+            for g in range(o.shape[0] // 16):
+                send[j, l * GROUPS + g, to, :] = o[16 * g : 16 * g + 16].astype(BF16)
 
         def post(k, _, j=j):
             t, copy = forward(j, k)
@@ -262,6 +278,21 @@
 
             return 0
 
+        def one(x, _):
+            store(0, x, along_y(x, (0,)))
+            return 0
+
+        def others(x, _):
+            o = along_y(x, (1, 2))
+            store(1, x, o[:, :LANES])
+            last = o[:, LANES:]
+            store(NORB, x, jnp.where(zone, last[:HALF], last[HALF:]))
+            return 0
+
+        along_z(0)
+        lax.fori_loop(0, NX, one, 0)
+        along_z(1)
+        lax.fori_loop(0, NX, others, 0)
         lax.fori_loop(0, GRANULES, post, 0)
 
     def reply(j, slot, k):
@@ -317,6 +348,10 @@
     for j in range(NSRC):
         got = back.at[j]
         pltpu.make_async_copy(got, got, rb.at[j]).wait()
+
+        def finish(l, m, value, j=j):
+            value = src[j, 400 * m : 400 * m + 400, :].astype(F32) * value
+            total[l, m] = value if j == 0 else total[l, m] + value
 
         def again_y(x, _, j=j):
             at = pl.ds(pl.multiple_of(x * 40, 8), 40)
@@ -339,25 +374,26 @@
                 t = dot(f, z_out[l, i])
                 here = t[:, :LANES] if left is None else left + t[:, :LANES]
                 left = t[:, LANES:]
-                dens[l, i] = srcd[j, i] * here if j == 0 else dens[l, i] + srcd[j, i] * here
-            dens[l, 4] = srcd[j, 4] * left if j == 0 else dens[l, 4] + srcd[j, 4] * left
+                finish(l, i, here)
+            finish(l, 4, left)
 
     def gather(x, _):
         at = pl.ds(pl.multiple_of(x * 40, 8), 40)
         for l in range(NORB):
             for m in range(5):
-                flat[pl.ds(NORB * (x * 200 + m) + l, 40, stride=5 * NORB), :] = -dens[l, m, at, :]
+                flat[pl.ds(NORB * (x * 200 + m) + l, 40, stride=5 * NORB), :] = -total[l, m, at, :]
         return 0
 
     lax.fori_loop(0, NX, gather, 0)
     out[...] = flat[...].reshape(SLAB, NORB, LANES).astype(BF16)
 
     for j in range(NSRC):
-        for k in range(1, 8):
+        swap(j).wait_send()
+        for k in range(1, 4):
             first(j, k).wait_send()
+            second(j, k).wait_send()
             third(j, k).wait_send()
-        for k in range(1, 4):
-            second(j, k).wait_send()
+        give(j).wait_send()
 
         def posted(k, _, j=j):
             t, copy = forward(j, k)
@@ -396,13 +432,15 @@
         out_specs=vmem,
         scratch_shapes=[
             pltpu.VMEM((NORB * SLAB, LANES), F32),
+            pltpu.VMEM((NORB, 5, 40 * NX, LANES), F32),
             pltpu.VMEM((NSRC, PADDED, LANES), BF16),
-            pltpu.VMEM((NSRC, 8, PIECE, LANES), BF16),
+            pltpu.VMEM((NSRC, PADDED // 2, LANES), BF16),
+            pltpu.VMEM((NSRC, PADDED // 2, LANES), BF16),
+            pltpu.VMEM((NSRC, 4, PIECE, LANES), BF16),
             pltpu.VMEM((NSRC, 4, PIECE, LANES), BF16),
             pltpu.VMEM((NSRC, PADDED, LANES), BF16),
-            pltpu.VMEM((PADDED, LANES), F32),
+            pltpu.VMEM((NORB, 5, 40 * NX, LANES), BF16),
             pltpu.VMEM((NORB, 5, 40 * NX, LANES), F32),
-            pltpu.VMEM((NSRC, 5, 40 * NX, LANES), F32),
             pltpu.VMEM((NORB + 1, 4, 40 * NX, LANES), F32),
             pltpu.VMEM((NSRC, GRANULES, PAIRROWS, LANES), BF16),
             pltpu.VMEM((NSRC, 2, NGRID, PAIRROWS, LANES), BF16),
@@ -410,11 +448,15 @@
             pltpu.VMEM((NSRC, 2, NGRID, PAIRROWS, LANES), BF16),
             pltpu.VMEM((NSRC, GRANULES, PAIRROWS, LANES), BF16),
             pltpu.VMEM((2 * NSRC, 16, N, LANES), F32),
-            dma((NSRC, 8)),
+            dma((NSRC,)),
             dma((NSRC, 4)),
-            dma((NSRC, 8)),
+            dma((NSRC, 4)),
+            dma((NSRC, 4)),
+            dma((NSRC,)),
             dma((NSRC, GRANULES)),
             dma((NSRC, 2, NGRID)),
+            dma((NSRC,)),
+            dma((NSRC,)),
             dma((NSRC,)),
             dma((NSRC,)),
             dma((NSRC,)),

time: 164 us -> 162 us (0.988)
  the two profiles are of different devices: /device:TPU:10 before, /device:TPU:93 now
where the time goes in v3:
time: 162 us; the launch traced here: 161 us
  Pallas kernels  159 us (98%)
  local copies, waits for them, and re-layouts  2.88 us (2%)
    pallas_call x1, Pallas kernels, exchange(): pl.pallas_call(body, out_shape=jax.ShapeDtypeStruct((SLAB, NORB, LANES),...  159 us

profile of v3, /device:TPU:93, one launch (start us, length us, event | category | flops | bytes accessed | tf_op | source)
XLA Modules:
  0.0 161.5 jit_solution(8928511407868143808)
XLA Ops:
  0.0 158.6 %exchange.1 = bf16[2000,2,128]{2,1,0:T(2,128)(2,1)} custom-call(s32[2]{0:T(128)} %index.1, bf16[2000,2,128]{2,1,0:T(2,128)(2,1)} %bitcast.7, bf16[160,160]{1,0:T(8,128)(2,1)} %constant.10.clone.cas, bf16[160,160]{1,0:T(8,128)(2,1)} %constant.11.clone.y_in, bf16[160,160]{1,0:T(8,128)(2,1)} %constant.12.clone.y_out, ...), custom_call_target="tpu_custom_call" | custom-call | tf_op jit(solution)/shard_map/exchange/pallas_call | solution.py:428
  158.6 2.9 %copy.9 = bf16[2,10,25600]{2,0,1:T(2,128)(2,1)} copy(bf16[2,10,25600]{2,0,1:T(2,128)(2,1)} %bitcast.6) | data formatting | bytes 2048000

commit v4 on v3

--- a/solution.py
+++ b/solution.py
@@ -124,73 +124,6 @@
     def granule(j, slot):
         return lax.rem(me + (NGRID - STEP) * j, NGRID) + NGRID * slot
 
-    pl.semaphore_wait(barrier, 1 + 3 + 3 + NGRID - 1)
-
-    def half(c):
-        return pl.ds(pl.multiple_of(c * (PADDED // 2), PADDED // 2), PADDED // 2)
-
-    def piece(x):
-        return pl.ds(pl.multiple_of(x * PIECE, PIECE), PIECE)
-
-    own = pl.ds(pl.multiple_of(core * (PADDED // 2) + x_at * PIECE, PIECE), PIECE)
-
-    def swap(j):
-        return pltpu.make_async_remote_copy(
-            con.at[j, half(1 - core)], bufd.at[j], sd.at[j], rd.at[j], device_id=twin, device_id_type=MESH)
-
-    def first(j, k):
-        x = lax.rem(x_at + k, 4)
-        return pltpu.make_async_remote_copy(
-            pair.at[j, piece(x)], buf1.at[j, x_at], s1.at[j, k], r1.at[j],
-            device_id=at_x(x), device_id_type=MESH)
-
-    def second(j, k):
-        y = lax.rem(y_at + k, 4)
-        return pltpu.make_async_remote_copy(
-            buf2.at[j, y_at], buf2.at[j, y_at], s2.at[j, k], r2.at[j],
-            device_id=at_y(y), device_id_type=MESH)
-
-    def third(j, k):
-        x = lax.rem(x_at + k, 4)
-        return pltpu.make_async_remote_copy(
-            src.at[j, own], src.at[j, own], s3.at[j, k], r3.at[j],
-            device_id=at_x(x), device_id_type=MESH)
-
-    def give(j):
-        ours = src.at[j, half(core)]
-        return pltpu.make_async_remote_copy(
-            ours, ours, se.at[j], re.at[j], device_id=twin, device_id_type=MESH)
-
-    def along_x1(j):
-        swap(j).wait_recv()
-        pair[j] = (con[j, half(core), :].astype(F32) + bufd[j].astype(F32)).astype(BF16)
-        for k in range(1, 4):
-            first(j, k).start()
-        buf1[j, x_at] = pair[j, piece(x_at), :]
-
-    def along_y1(j):
-        got = buf1.at[j, pl.ds(0, 3)]
-        pltpu.make_async_copy(got, got, r1.at[j]).wait()
-        buf2[j, y_at] = jnp.sum(buf1[j].astype(F32), axis=0).astype(BF16)
-        for k in range(1, 4):
-            second(j, k).start()
-
-    def along_x2(j):
-        got = buf2.at[j, pl.ds(0, 3)]
-        pltpu.make_async_copy(got, got, r2.at[j]).wait()
-        src[j, own, :] = jnp.sum(buf2[j].astype(F32), axis=0).astype(BF16)
-        for k in range(1, 4):
-            third(j, k).start()
-
-    def to_twin(j):
-        got = src.at[j, pl.ds(0, 3 * PIECE)]
-        pltpu.make_async_copy(got, got, r3.at[j]).wait()
-        give(j).start()
-
-    swap(0).start()
-    swap(1).start()
-    along_x1(0)
-
     lane = lax.broadcasted_iota(jnp.int32, (1, LANES), 1)
     kx = squares(lax.broadcasted_iota(jnp.int32, (N, LANES), 0))
     strength = (N * SPACING) ** 2 / math.pi
@@ -209,6 +142,73 @@
                 return 0
 
             lax.fori_loop(0, 16, fill, 0)
+
+    pl.semaphore_wait(barrier, 1 + 3 + 3 + NGRID - 1)
+
+    def half(c):
+        return pl.ds(pl.multiple_of(c * (PADDED // 2), PADDED // 2), PADDED // 2)
+
+    def piece(x):
+        return pl.ds(pl.multiple_of(x * PIECE, PIECE), PIECE)
+
+    own = pl.ds(pl.multiple_of(core * (PADDED // 2) + x_at * PIECE, PIECE), PIECE)
+
+    def swap(j):
+        return pltpu.make_async_remote_copy(
+            con.at[j, half(1 - core)], bufd.at[j], sd.at[j], rd.at[j], device_id=twin, device_id_type=MESH)
+
+    def first(j, k):
+        x = lax.rem(x_at + k, 4)
+        return pltpu.make_async_remote_copy(
+            pair.at[j, piece(x)], buf1.at[j, x_at], s1.at[j, k], r1.at[j],
+            device_id=at_x(x), device_id_type=MESH)
+
+    def second(j, k):
+        y = lax.rem(y_at + k, 4)
+        return pltpu.make_async_remote_copy(
+            buf2.at[j, y_at], buf2.at[j, y_at], s2.at[j, k], r2.at[j],
+            device_id=at_y(y), device_id_type=MESH)
+
+    def third(j, k):
+        x = lax.rem(x_at + k, 4)
+        return pltpu.make_async_remote_copy(
+            src.at[j, own], src.at[j, own], s3.at[j, k], r3.at[j],
+            device_id=at_x(x), device_id_type=MESH)
+
+    def give(j):
+        ours = src.at[j, half(core)]
+        return pltpu.make_async_remote_copy(
+            ours, ours, se.at[j], re.at[j], device_id=twin, device_id_type=MESH)
+
+    def along_x1(j):
+        swap(j).wait_recv()
+        pair[j] = (con[j, half(core), :].astype(F32) + bufd[j].astype(F32)).astype(BF16)
+        for k in range(1, 4):
+            first(j, k).start()
+        buf1[j, x_at] = pair[j, piece(x_at), :]
+
+    def along_y1(j):
+        got = buf1.at[j, pl.ds(0, 3)]
+        pltpu.make_async_copy(got, got, r1.at[j]).wait()
+        buf2[j, y_at] = jnp.sum(buf1[j].astype(F32), axis=0).astype(BF16)
+        for k in range(1, 4):
+            second(j, k).start()
+
+    def along_x2(j):
+        got = buf2.at[j, pl.ds(0, 3)]
+        pltpu.make_async_copy(got, got, r2.at[j]).wait()
+        src[j, own, :] = jnp.sum(buf2[j].astype(F32), axis=0).astype(BF16)
+        for k in range(1, 4):
+            third(j, k).start()
+
+    def to_twin(j):
+        got = src.at[j, pl.ds(0, 3 * PIECE)]
+        pltpu.make_async_copy(got, got, r3.at[j]).wait()
+        give(j).start()
+
+    swap(0).start()
+    swap(1).start()
+    along_x1(0)
 
     along_y1(0)
     along_x1(1)

time: 162 us -> 160 us (0.988)
  the two profiles are of different devices: /device:TPU:93 before, /device:TPU:54 now
where the time goes in v4:
time: 160 us
  Pallas kernels  157 us (98%)
  local copies, waits for them, and re-layouts  2.88 us (2%)
    pallas_call x1, Pallas kernels, exchange(): pl.pallas_call(body, out_shape=jax.ShapeDtypeStruct((SLAB, NORB, LANES),...  157 us

profile of v4, /device:TPU:54, one launch (start us, length us, event | category | flops | bytes accessed | tf_op | source)
XLA Modules:
  0.0 160.2 jit_solution(12831368403845096689)
XLA Ops:
  0.0 157.3 %exchange.1 = bf16[2000,2,128]{2,1,0:T(2,128)(2,1)} custom-call(s32[2]{0:T(128)} %index.1, bf16[2000,2,128]{2,1,0:T(2,128)(2,1)} %bitcast.7, bf16[160,160]{1,0:T(8,128)(2,1)} %constant.10.clone.cas, bf16[160,160]{1,0:T(8,128)(2,1)} %constant.11.clone.y_in, bf16[160,160]{1,0:T(8,128)(2,1)} %constant.12.clone.y_out, ...), custom_call_target="tpu_custom_call" | custom-call | tf_op jit(solution)/shard_map/exchange/pallas_call | solution.py:428
  157.3 2.9 %copy.9 = bf16[2,10,25600]{2,0,1:T(2,128)(2,1)} copy(bf16[2,10,25600]{2,0,1:T(2,128)(2,1)} %bitcast.6) | data formatting | bytes 2048000

commit v5 on v4

--- a/solution.py
+++ b/solution.py
@@ -381,7 +381,7 @@
         at = pl.ds(pl.multiple_of(x * 40, 8), 40)
         for l in range(NORB):
             for m in range(5):
-                flat[pl.ds(NORB * (x * 200 + m) + l, 40, stride=5 * NORB), :] = -total[l, m, at, :]
+                flat[pl.ds(NORB * (x * 200 + m) + l, 40, stride=5 * NORB), :] = total[l, m, at, :]
         return 0
 
     lax.fori_loop(0, NX, gather, 0)
@@ -473,7 +473,7 @@
 def shards(orbitals, source_index):
     rows = orbitals.reshape(NORB, SLAB, LANES).transpose(1, 0, 2)
     result = exchange(source_index, rows)
-    return result.transpose(1, 0, 2).reshape(orbitals.shape)
+    return -result.transpose(1, 0, 2).reshape(orbitals.shape)
 
 
 def solution(mesh):

time: 160 us -> 160 us (level)
  local copies, waits for them, and re-layouts: 2.88 us -> 0 us
  other arithmetic: 0 us -> 2.77 us
    unnamed x1 -> x0, local copies, waits for them, and re-layouts: 2.88 us -> none
    neg x0 -> x1, other arithmetic: none -> 2.77 us  [shards(): return -result.transpose(1, 0, 2).reshape(orbitals.shape)]
where the time goes in v5:
time: 160 us
  Pallas kernels  157 us (98%)
  other arithmetic  2.77 us (2%)
    pallas_call x1, Pallas kernels, exchange(): pl.pallas_call(body, out_shape=jax.ShapeDtypeStruct((SLAB, NORB, LANES),...  157 us

profile of v5, /device:TPU:54, one launch (start us, length us, event | category | flops | bytes accessed | tf_op | source)
XLA Modules:
  0.0 160.0 jit_solution(10540065202388928536)
XLA Ops:
  0.0 157.2 %exchange.1 = bf16[2000,2,128]{2,1,0:T(2,128)(2,1)} custom-call(s32[2]{0:T(128)} %index.1, bf16[2000,2,128]{2,1,0:T(2,128)(2,1)} %bitcast.6, bf16[160,160]{1,0:T(8,128)(2,1)} %constant.10.clone.cas, bf16[160,160]{1,0:T(8,128)(2,1)} %constant.11.clone.y_in, bf16[160,160]{1,0:T(8,128)(2,1)} %constant.12.clone.y_out, ...), custom_call_target="tpu_custom_call" | custom-call | tf_op jit(solution)/shard_map/exchange/pallas_call | solution.py:428
  157.2 2.8 %neg.9 = bf16[2000,2,128]{2,1,0:T(2,128)(2,1)} negate(bf16[2000,2,128]{2,1,0:T(2,128)(2,1)} %exchange.1) | non-fusion elementwise | flops 512000 | bytes 2048000 | tf_op jit(solution)/shard_map/neg | solution.py:476
